TPU v7x, 128 devices: a whole 4x4x4 slice. The times are simulated.
128 devices in a mesh: expert: 16 (over y, x), edata: 8 (over z, core).
Axes of the slice: x: 4, y: 4, z: 4, core: 2. Of those that a mesh axis runs over, the one named last changes fastest.
Arguments:
- out_grad: bfloat16 [131072, 4096], P(('expert', 'edata')), may hold values from -3.5 to 3.5
- hidden_saved: bfloat16 [131072, 768], P(('expert', 'edata')), may hold values from -6 to 6
- recv_counts: int32 [2048], P(('expert', 'edata')), may hold values from 1 to 64, as said below
- master_weight: float32 [65536, 768], P(('expert', 'edata'))
- moment_one: bfloat16 [65536, 768], P(('expert', 'edata')), may hold values from -4 to 4
- moment_two: bfloat16 [65536, 768], P(('expert', 'edata')), may hold values from 0.049804688 to 0.5
Outputs:
- new_master: float32 [65536, 768], P(('expert', 'edata'))
- new_moment_one: bfloat16 [65536, 768], P(('expert', 'edata'))
- new_moment_two: bfloat16 [65536, 768], P(('expert', 'edata'))
- scaled_weight: bfloat16 [65536, 768], P('expert')
- expert_peak: float32 [16], P('expert')
Inputs may be any that keep to these rules, and one draw needn't show every extreme that they name: `recv_counts`: counts are skewed over experts; in every draw some pair fills all 64 slots.
All inputs are finite; a program needn't handle non-finite values. Where the computation divides by a largest or mean magnitude, that divisor is 1e-20 or more.
Results may differ from a plain program's by a relative error of at most 0.001.
Values may be sent and summed in bfloat16 or wider, within the bound.
A program may use at most 128 MiB of HBM per device.

v0:
```python
import jax
import jax.numpy as jnp
from jax import lax
from jax.sharding import PartitionSpec as P

beta_one = 0.9
beta_two = 0.999
correct_one = 1.0 - 0.9**5
correct_two = 1.0 - 0.999**5
adam_eps = 1e-08
learn_rate = 0.05
weight_decay = 1.0
peak_eps = 1e-06


def local(out_grad, hidden_saved, recv_counts, master_weight, moment_one, moment_two):
    experts = lax.axis_size("expert")
    capacity = out_grad.shape[0] // experts
    arrived = lax.all_to_all(out_grad, "expert", split_axis=0, concat_axis=0, tiled=True)
    slots = jnp.arange(capacity)
    live = (slots[None, :] < recv_counts[:, None]).reshape(-1)
    masked = jnp.where(live[:, None], arrived, jnp.zeros((), jnp.bfloat16))
    grad = lax.psum_scatter(
        lax.dot_general(
            masked, hidden_saved, (((0,), (0,)), ((), ())), preferred_element_type=jnp.float32
        ),
        "edata",
        scatter_dimension=0,
        tiled=True,
    )
    first = beta_one * moment_one.astype(jnp.float32) + (1.0 - beta_one) * grad
    second = beta_two * moment_two.astype(jnp.float32) + (1.0 - beta_two) * grad * grad
    update = first / correct_one / (jnp.sqrt(second / correct_two) + adam_eps)
    new_master = master_weight - learn_rate * (update + weight_decay * master_weight)
    local_peak = jnp.max(jnp.abs(new_master))
    peak = lax.pmax(local_peak, "edata")
    scaled_shard = (new_master / (peak + peak_eps)).astype(jnp.bfloat16)
    scaled = lax.all_gather(scaled_shard, "edata", axis=0, tiled=True)
    return (
        new_master,
        first.astype(jnp.bfloat16),
        second.astype(jnp.bfloat16),
        scaled,
        peak.reshape(1),
    )


def solution(mesh):
    placed = (
        P(("expert", "edata"), None),
        P(("expert", "edata"), None),
        P(("expert", "edata")),
        P(("expert", "edata"), None),
        P(("expert", "edata"), None),
        P(("expert", "edata"), None),
    )
    return jax.shard_map(
        local,
        mesh=mesh,
        in_specs=placed,
        out_specs=(
            P(("expert", "edata"), None),
            P(("expert", "edata"), None),
            P(("expert", "edata"), None),
            P("expert", None),
            P("expert"),
        ),
        check_vma=False,
    )
```

profile of v0, /device:TPU:1, one launch (start us, length us, event | category | flops | bytes accessed | tf_op | source)
XLA Modules:
  0.0 306.5 jit_solution(4694745972800328352)
XLA Ops:
  7.2 0.0 copy-start
  7.2 0.0 copy-start.2
  7.2 7.8 %all-to-all-start = ((bf16[16,64,4096]{2,1,0:T(8,128)(2,1)}), bf16[16,64,4096]{2,1,0:T(8,128)(2,1)}, u32[]{:S(2)}, u32[]{:S(2)}) async-start(bf16[16,64,4096]{2,1,0:T(8,128)(2,1)} %bitcast.6), calls=%async_computation | async-start | bytes 16777216 | tf_op jit(solution)/shard_map/all_to_all | solution.py:19
  15.0 0.0 reduce-scatter.2.cloned.1.call-start
  15.0 0.0 copy-done.2
  15.0 0.1 iota_compare_fusion
  15.1 0.1 lt.23
  15.2 123.1 %all-to-all-done = bf16[16,64,4096]{2,1,0:T(8,128)(2,1)} async-done(((bf16[16,64,4096]{2,1,0:T(8,128)(2,1)}), bf16[16,64,4096]{2,1,0:T(8,128)(2,1)}, u32[]{:S(2)}, u32[]{:S(2)}) %all-to-all-start) | async-done | bytes 8388640 | tf_op jit(solution)/shard_map/all_to_all | solution.py:19
  138.3 7.2 %bitcast_select_fusion = bf16[1024,4096]{1,0:T(8,128)(2,1)} fusion(bf16[16,64,4096]{2,1,0:T(8,128)(2,1)} %all-to-all-done, pred[1024]{0:T(1024)(128)(4,1)S(1)} %lt.23), kind=kLoop, calls=%fused_computation | loop fusion | flops 4194304 | bytes 16778240 | tf_op jit(solution)/shard_map/jit(_where)/select_n | solution.py:22
  145.5 0.0 copy-done
  145.5 12.9 %fusion.3 = f32[4096,768]{1,0:T(8,128)} fusion(bf16[1024,4096]{1,0:T(8,128)(2,1)} %bitcast_select_fusion, bf16[1024,768]{1,0:T(8,128)(2,1)S(1)} %copy-done), kind=kOutput, calls=%fused_computation.10 | convolution fusion | flops 6442450944 | bytes 22544384 | tf_op jit(solution)/shard_map/dot_general | solution.py:24
  158.4 0.0 reduce-scatter.2.cloned.1.call-update
  158.4 0.0 all-gather.2.cloned.1.call-start
  158.5 74.1 %reduce-scatter.2.cloned.1.call-done = f32[512,768]{1,0:T(8,128)} async-done(((f32[4096,768]{1,0:T(8,128)}), f32[512,768]{1,0:T(8,128)}) %reduce-scatter.2.cloned.1.call-update) | async-done | bytes 1572880 | tf_op jit(solution)/shard_map/reduce_scatter | solution.py:23
  232.5 5.4 %abs_reduce_fusion = (f32[]{:T(128)}, f32[512,768]{1,0:T(8,128)S(1)}, bf16[512,768]{1,0:T(8,128)(2,1)}, bf16[512,768]{1,0:T(8,128)(2,1)}) fusion(f32[512,768]{1,0:T(8,128)} %param.9, f32[512,768]{1,0:T(8,128)} %reduce-scatter.2.cloned.1.call-done, bf16[512,768]{1,0:T(8,128)(2,1)} %param.11, bf16[512,768]{1,0:T(8,128)(2,1)} %param.10), kind=kLoop, calls=%fused_computation.4 | loop fusion | flops 7864319 | bytes 7864324 | tf_op jit(solution)/shard_map/reduce_max | solution.py:35
  238.0 0.0 copy-start.1
  238.0 13.8 %pmax.7 = f32[]{:T(128)} all-reduce(f32[]{:T(128)} %get-tuple-element.5), channel_id=1, replica_groups=mesh['expert'=16,'edata'=8] {'edata'}, use_global_device_ids=true, to_apply=%region_2.3 | all-reduce | flops 1 | bytes 8 | tf_op jit(solution)/shard_map/pmax | solution.py:36
  252.4 1.0 divide_convert_fusion
  253.4 0.0 all-gather.2.cloned.1.call-update
  253.4 0.0 copy-done.1
  253.4 40.4 %all-gather.2.cloned.1.call-done = bf16[4096,768]{1,0:T(8,128)(2,1)} async-done(((bf16[512,768]{1,0:T(8,128)(2,1)}), bf16[4096,768]{1,0:T(8,128)(2,1)}) %all-gather.2.cloned.1.call-update) | async-done | bytes 6291472 | tf_op jit(solution)/shard_map/all_gather | solution.py:38
  293.8 5.9 %copy.12 = bf16[4096,768]{1,0:T(8,128)(2,1)} copy(bf16[4096,768]{1,0:T(8,128)(2,1)} %all-gather.2.cloned.1.call-done) | data formatting | bytes 12582912
Async XLA Ops:
  7.2 138.4 %copy-start = (bf16[1024,768]{1,0:T(8,128)(2,1)S(1)}, bf16[1024,768]{1,0:T(8,128)(2,1)}, u32[]{:S(2)}) copy-start(bf16[1024,768]{1,0:T(8,128)(2,1)} %param.7) | copy-start | bytes 4718596
  7.2 7.8 %copy-start.2 = (s32[16]{0:T(128)S(1)}, s32[16]{0:T(128)}, u32[]{:S(2)}) copy-start(s32[16]{0:T(128)} %param.8) | copy-start | bytes 196
  7.2 131.1 %all-to-all-start = ((bf16[16,64,4096]{2,1,0:T(8,128)(2,1)}), bf16[16,64,4096]{2,1,0:T(8,128)(2,1)}, u32[]{:S(2)}, u32[]{:S(2)}) async-start(bf16[16,64,4096]{2,1,0:T(8,128)(2,1)} %bitcast.6), calls=%async_computation | async-start | bytes 16777216 | tf_op jit(solution)/shard_map/all_to_all | solution.py:19
  15.0 217.6 %reduce-scatter.2.cloned.1.call-start = ((), (), s32[]{:S(2)}) async-start(), calls=%async_computation.2 | async-start | bytes 14155776 | tf_op jit(solution)/shard_map/reduce_scatter | solution.py:23
  158.4 135.4 %all-gather.2.cloned.1.call-start = ((), (), s32[]{:S(2)}) async-start(), calls=%async_computation.3 | async-start | bytes 7077888 | tf_op jit(solution)/shard_map/all_gather | solution.py:38
  238.0 15.4 %copy-start.1 = (f32[512,768]{1,0:T(8,128)}, f32[512,768]{1,0:T(8,128)S(1)}, u32[]{:S(2)}) copy-start(f32[512,768]{1,0:T(8,128)S(1)} %get-tuple-element.14) | copy-start | bytes 4718596
Sparse Core Ops, SparseCore 0:
  158.5 73.9 reduce-scatter.1
  253.5 40.2 all-gather.1
where the time goes:
time: 307 us
  waiting for transfers between devices  238 us (78%)
  between operations  14.7 us (5%)
  blocking collectives  13.8 us (4%)
  other arithmetic  13.7 us (4%)
  matrix products  12.9 us (4%)
  starting transfers between devices  7.85 us (3%)
  local copies, waits for them, and re-layouts  6 us (2%)
    all_to_all x1, waiting for transfers between devices, local(): lax.all_to_all(out_grad, 'expert', split_axis=0, concat_axis=0, tiled=True)  123 us
    reduce_scatter x1, waiting for transfers between devices, local(): lax.psum_scatter(lax.dot_general(masked, hidden_saved, (((0,), (0,)), (()...  74.1 us
    all_gather x1, waiting for transfers between devices, local(): scaled = lax.all_gather(scaled_shard, 'edata', axis=0, tiled=True)  40.4 us
    pmax x1, blocking collectives, local(): peak = lax.pmax(local_peak, 'edata')  13.8 us
    dot_general x1, matrix products, local(): lax.dot_general(masked, hidden_saved, (((0,), (0,)), ((), ())), preferred...  12.9 us
    all_to_all x1, starting transfers between devices, local(): lax.all_to_all(out_grad, 'expert', split_axis=0, concat_axis=0, tiled=True)  7.77 us
    select_n x1, other arithmetic, local(): masked = jnp.where(live[:, None], arrived, jnp.zeros((), jnp.bfloat16))  7.22 us
  transfers between devices with their start and end apart: 3, of which 3 were waited for; matrix products, arithmetic and copies ran while one was open for 0% of the time, Pallas kernels for 0%

commit v1 on v0

--- a/solution.py
+++ b/solution.py
@@ -35,7 +35,9 @@
     local_peak = jnp.max(jnp.abs(new_master))
     peak = lax.pmax(local_peak, "edata")
     scaled_shard = (new_master / (peak + peak_eps)).astype(jnp.bfloat16)
-    scaled = lax.all_gather(scaled_shard, "edata", axis=0, tiled=True)
+    scaled = jnp.concatenate(
+        lax.all_to_all(jnp.stack([scaled_shard] * lax.axis_size("edata")), "edata", 0, 0), axis=0
+    )
     return (
         new_master,
         first.astype(jnp.bfloat16),

time: 307 us -> 337 us (1.098)
  blocking collectives: 13.8 us -> 88.1 us
  waiting for transfers between devices: 238 us -> 197 us
    all_to_all x0 -> x1, blocking collectives: none -> 74.3 us  [local(): lax.all_to_all(jnp.stack([scaled_shard] * lax.axis_size('edata')), 'edata...]
    all_gather x1 -> x0, waiting for transfers between devices: 40.4 us -> none  [local(): scaled = lax.all_gather(scaled_shard, 'edata', axis=0, tiled=True)]
  transfers between devices with their start and end apart: 3 -> 2, of which waited for: 3 -> 2; matrix products, arithmetic and copies ran while one was open for 0% -> 0% of each run, Pallas kernels for 0% -> 0%
where the time goes in v1:
time: 337 us
  waiting for transfers between devices  197 us (58%)
  blocking collectives  88.1 us (26%)
  between operations  14.7 us (4%)
  matrix products  12.9 us (4%)
  other arithmetic  12.8 us (4%)
  starting transfers between devices  7.81 us (2%)
    all_to_all x1, waiting for transfers between devices, local(): lax.all_to_all(out_grad, 'expert', split_axis=0, concat_axis=0, tiled=True)  123 us
    all_to_all x1, blocking collectives, local(): lax.all_to_all(jnp.stack([scaled_shard] * lax.axis_size('edata')), 'edata...  74.3 us
    reduce_scatter x1, waiting for transfers between devices, local(): lax.psum_scatter(lax.dot_general(masked, hidden_saved, (((0,), (0,)), (()...  74.1 us
    pmax x1, blocking collectives, local(): peak = lax.pmax(local_peak, 'edata')  13.8 us
    dot_general x1, matrix products, local(): lax.dot_general(masked, hidden_saved, (((0,), (0,)), ((), ())), preferred...  12.9 us
    all_to_all x1, starting transfers between devices, local(): lax.all_to_all(out_grad, 'expert', split_axis=0, concat_axis=0, tiled=True)  7.77 us
    select_n x1, other arithmetic, local(): masked = jnp.where(live[:, None], arrived, jnp.zeros((), jnp.bfloat16))  7.21 us
  transfers between devices with their start and end apart: 2, of which 2 were waited for; matrix products, arithmetic and copies ran while one was open for 0% of the time, Pallas kernels for 0%

profile of v1, /device:TPU:1, one launch (start us, length us, event | category | flops | bytes accessed | tf_op | source)
XLA Modules:
  0.0 336.8 jit_solution(9706345110864537874)
XLA Ops:
  7.2 0.0 copy-start
  7.2 0.0 copy-start.2
  7.2 7.8 %all-to-all-start = ((bf16[16,64,4096]{2,1,0:T(8,128)(2,1)}), bf16[16,64,4096]{2,1,0:T(8,128)(2,1)}, u32[]{:S(2)}, u32[]{:S(2)}) async-start(bf16[16,64,4096]{2,1,0:T(8,128)(2,1)} %bitcast.8), calls=%async_computation | async-start | bytes 16777216 | tf_op jit(solution)/shard_map/all_to_all | solution.py:19
  15.0 0.0 reduce-scatter.2.cloned.1.call-start
  15.0 0.0 copy-done.2
  15.0 0.1 iota_compare_fusion
  15.1 0.1 lt.23
  15.2 123.1 %all-to-all-done = bf16[16,64,4096]{2,1,0:T(8,128)(2,1)} async-done(((bf16[16,64,4096]{2,1,0:T(8,128)(2,1)}), bf16[16,64,4096]{2,1,0:T(8,128)(2,1)}, u32[]{:S(2)}, u32[]{:S(2)}) %all-to-all-start) | async-done | bytes 8388640 | tf_op jit(solution)/shard_map/all_to_all | solution.py:19
  138.3 7.2 %bitcast_select_fusion = bf16[1024,4096]{1,0:T(8,128)(2,1)} fusion(bf16[16,64,4096]{2,1,0:T(8,128)(2,1)} %all-to-all-done, pred[1024]{0:T(1024)(128)(4,1)S(1)} %lt.23), kind=kLoop, calls=%fused_computation | loop fusion | flops 4194304 | bytes 16778240 | tf_op jit(solution)/shard_map/jit(_where)/select_n | solution.py:22
  145.5 0.0 copy-done
  145.5 12.9 %fusion.3 = f32[4096,768]{1,0:T(8,128)} fusion(bf16[1024,4096]{1,0:T(8,128)(2,1)} %bitcast_select_fusion, bf16[1024,768]{1,0:T(8,128)(2,1)S(1)} %copy-done), kind=kOutput, calls=%fused_computation.10 | convolution fusion | flops 6442450944 | bytes 22544384 | tf_op jit(solution)/shard_map/dot_general | solution.py:24
  158.4 0.0 reduce-scatter.2.cloned.1.call-update
  158.4 74.1 %reduce-scatter.2.cloned.1.call-done = f32[512,768]{1,0:T(8,128)} async-done(((f32[4096,768]{1,0:T(8,128)}), f32[512,768]{1,0:T(8,128)}) %reduce-scatter.2.cloned.1.call-update) | async-done | bytes 1572880 | tf_op jit(solution)/shard_map/reduce_scatter | solution.py:23
  232.5 5.4 %abs_reduce_fusion = (f32[]{:T(128)}, f32[512,768]{1,0:T(8,128)S(1)}, bf16[512,768]{1,0:T(8,128)(2,1)}, bf16[512,768]{1,0:T(8,128)(2,1)}) fusion(f32[512,768]{1,0:T(8,128)} %param.9, f32[512,768]{1,0:T(8,128)} %reduce-scatter.2.cloned.1.call-done, bf16[512,768]{1,0:T(8,128)(2,1)} %param.11, bf16[512,768]{1,0:T(8,128)(2,1)} %param.10), kind=kLoop, calls=%fused_computation.4 | loop fusion | flops 7864319 | bytes 7864324 | tf_op jit(solution)/shard_map/reduce_max | solution.py:35
  238.0 0.0 copy-start.1
  238.0 13.8 %pmax.7 = f32[]{:T(128)} all-reduce(f32[]{:T(128)} %get-tuple-element.5), channel_id=1, replica_groups=mesh['expert'=16,'edata'=8] {'edata'}, use_global_device_ids=true, to_apply=%region_2.3 | all-reduce | flops 1 | bytes 8 | tf_op jit(solution)/shard_map/pmax | solution.py:36
  252.4 0.1 divide_convert_fusion
  252.5 0.4 stack.2
  252.9 0.0 copy-done.1
  252.9 74.3 %all_to_all.17 = bf16[8,512,768]{2,1,0:T(8,128)(2,1)S(1)} all-to-all(bf16[8,512,768]{2,1,0:T(8,128)(2,1)S(1)} %stack.2), channel_id=1, replica_groups=mesh['expert'=16,'edata'=8] {'edata'}, dimensions={0} | all-to-all | bytes 12582912 | tf_op jit(solution)/shard_map/all_to_all | solution.py:39
  327.2 2.7 copy.12
Async XLA Ops:
  7.2 138.4 %copy-start = (bf16[1024,768]{1,0:T(8,128)(2,1)S(1)}, bf16[1024,768]{1,0:T(8,128)(2,1)}, u32[]{:S(2)}) copy-start(bf16[1024,768]{1,0:T(8,128)(2,1)} %param.7) | copy-start | bytes 4718596
  7.2 7.8 %copy-start.2 = (s32[16]{0:T(128)S(1)}, s32[16]{0:T(128)}, u32[]{:S(2)}) copy-start(s32[16]{0:T(128)} %param.8) | copy-start | bytes 196
  7.2 131.1 %all-to-all-start = ((bf16[16,64,4096]{2,1,0:T(8,128)(2,1)}), bf16[16,64,4096]{2,1,0:T(8,128)(2,1)}, u32[]{:S(2)}, u32[]{:S(2)}) async-start(bf16[16,64,4096]{2,1,0:T(8,128)(2,1)} %bitcast.8), calls=%async_computation | async-start | bytes 16777216 | tf_op jit(solution)/shard_map/all_to_all | solution.py:19
  15.0 217.6 %reduce-scatter.2.cloned.1.call-start = ((), (), s32[]{:S(2)}) async-start(), calls=%async_computation.3 | async-start | bytes 14155776 | tf_op jit(solution)/shard_map/reduce_scatter | solution.py:23
  238.0 15.0 %copy-start.1 = (f32[512,768]{1,0:T(8,128)}, f32[512,768]{1,0:T(8,128)S(1)}, u32[]{:S(2)}) copy-start(f32[512,768]{1,0:T(8,128)S(1)} %get-tuple-element.14) | copy-start | bytes 4718596
Sparse Core Ops, SparseCore 0:
  158.5 73.9 reduce-scatter.1
